TPU v7x, 32 devices: a whole 2x2x4 slice. The times are simulated.
32 devices in a mesh: shard: 4 (over z), ctx: 4 (over y, x), tensor: 2 (over core).
Axes of the slice: x: 2, y: 2, z: 4, core: 2. Of those that a mesh axis runs over, the one named last changes fastest.
Arguments:
- inputs: bfloat16 [2, 1280, 1472], P(None, ('shard', 'ctx')), may hold values from -6 to 6
- cotangent: bfloat16 [2, 1280, 1472], P(None, ('shard', 'ctx')), may hold values from -6 to 6
- norm1_gain: bfloat16 [1472], P('shard'), may hold values from 0.099609375 to 1.8984375
- w_query: bfloat16 [1472, 384], P('shard', 'tensor'), may hold values from -0.0390625 to 0.0390625
- w_key: bfloat16 [1472, 384], P('shard', 'tensor'), may hold values from -0.15625 to 0.15625
- w_value: bfloat16 [1472, 384], P('shard', 'tensor'), may hold values from -0.15625 to 0.15625
- w_out: bfloat16 [384, 1472], P('tensor', 'shard'), may hold values from -1.25 to 1.25
- norm2_gain: bfloat16 [1472], P('shard'), may hold values from 0.099609375 to 1.8984375
- w_gate: bfloat16 [1472, 3584], P('shard', 'tensor'), may hold values from -0.15625 to 0.15625
- w_up: bfloat16 [1472, 3584], P('shard', 'tensor'), may hold values from -0.15625 to 0.15625
- w_down: bfloat16 [3584, 1472], P('tensor', 'shard'), may hold values from -0.1875 to 0.1875
- bias_table: float32 [32, 6], replicated, may hold values from -4 to 4
Outputs:
- output: bfloat16 [2, 1280, 1472], P(None, ('shard', 'ctx'))
- input_grad: bfloat16 [2, 1280, 1472], P(None, ('shard', 'ctx'))
- norm1_gain_grad: float32 [1472], P('shard')
- w_query_grad: float32 [1472, 384], P('shard', 'tensor')
- w_key_grad: float32 [1472, 384], P('shard', 'tensor')
- w_value_grad: float32 [1472, 384], P('shard', 'tensor')
- w_out_grad: float32 [384, 1472], P('tensor', 'shard')
- norm2_gain_grad: float32 [1472], P('shard')
- w_gate_grad: float32 [1472, 3584], P('shard', 'tensor')
- w_up_grad: float32 [1472, 3584], P('shard', 'tensor')
- w_down_grad: float32 [3584, 1472], P('tensor', 'shard')
All inputs are finite; a program needn't handle non-finite values.
Results may differ from a plain program's by a relative error of at most 0.024.
Values may be sent and summed in bfloat16 or wider, within the bound.
No kernel may reach another device: no remote copies, remote signals or barrier semaphores. Data moves between devices by JAX's collectives and lax.ppermute only.
A program may use at most 128 MiB of HBM per device.

v0:
```python
import jax
import jax.numpy as jnp
from jax import lax
from jax.sharding import PartitionSpec as P

DK = 64
norm_eps = 1e-06
distance_marks = (8, 12, 16, 23, 32, 46, 64, 91)
masked_score = -1e30


def for_sending(x):
    return jax.tree.map(lambda a: a.astype(jnp.bfloat16) if a.dtype == jnp.float32 else a, x)


def path_info(token, seg_len):
    segment = jnp.where(
        token < 8 * seg_len,
        0,
        jnp.where(
            token < 12 * seg_len,
            (token - 8 * seg_len) // seg_len + 1,
            (token - 12 * seg_len) // seg_len + 5,
        ),
    )
    parent = jnp.where(segment == 0, -1, jnp.where(segment <= 4, 0, (segment - 5) // 2 + 1))
    place = token - jnp.where(
        segment == 0, 0, jnp.where(segment <= 4, (segment - 1) * seg_len, (segment - 2) * seg_len)
    )
    return (segment, parent, place)


def bucket_of(relative):
    magnitude = jnp.abs(relative)
    marked = sum(((magnitude >= mark).astype(jnp.int32) for mark in distance_marks))
    return jnp.where(relative > 0, 16, 0) + jnp.where(magnitude < 8, magnitude, 7 + marked)


def score_bias(query_token, key_token, table, seg_len):
    query_seg, query_parent, query_place = path_info(query_token, seg_len)
    key_seg, key_parent, key_place = path_info(key_token, seg_len)
    allowed = (
        (key_seg[None, :] == 0)
        | (key_seg[None, :] == query_seg[:, None])
        | (key_seg[None, :] == query_parent[:, None])
    )
    bucket = bucket_of(key_place[None, :] - query_place[:, None])
    looked = jnp.stack([jnp.take(table[:, head], bucket, axis=0) for head in range(table.shape[1])])
    return jnp.where(allowed[None], looked, masked_score)


def left_dot(left, right):
    return lax.dot_general(
        left, right, (((0,), (0,)), ((), ())), preferred_element_type=jnp.float32
    )


def right_dot(left, right):
    return lax.dot_general(
        left, right, (((1,), (1,)), ((), ())), preferred_element_type=jnp.float32
    )


def norm_back(values_in, scale, gain, normed_grad):
    weighted = normed_grad * gain
    value_grad = scale * weighted - values_in * scale**3 * jnp.mean(
        weighted * values_in, axis=-1, keepdims=True
    )
    gain_grad = jnp.sum(normed_grad * values_in * scale, axis=0)
    return (value_grad, gain_grad)


def gelu_tanh(value_in):
    return jax.nn.gelu(value_in, approximate=True)


def one_layer(weights, tokens_in, grad_in, bias_local, row_count, key_count):
    gain_one, w_query, w_key, w_value, w_out, gain_two, w_gate, w_up, w_down = weights
    inner = w_query.shape[1]
    heads_local = inner // DK
    gain_first = gain_one.astype(jnp.float32)
    gain_second = gain_two.astype(jnp.float32)
    start_in = tokens_in.astype(jnp.float32)
    scale_one = lax.rsqrt(jnp.mean(start_in * start_in, axis=-1, keepdims=True) + norm_eps)
    normed_one = (start_in * scale_one * gain_first).astype(jnp.bfloat16)
    queries = jnp.dot(normed_one, w_query, preferred_element_type=jnp.float32).astype(jnp.bfloat16)
    keys = jnp.dot(normed_one, w_key, preferred_element_type=jnp.float32).astype(jnp.bfloat16)
    values = jnp.dot(normed_one, w_value, preferred_element_type=jnp.float32).astype(jnp.bfloat16)
    key_path, value_path = (
        lax.all_gather(keys, "ctx", axis=0, tiled=True),
        lax.all_gather(values, "ctx", axis=0, tiled=True),
    )
    query_heads = queries.reshape(row_count, heads_local, DK)
    key_heads = key_path.reshape(key_count, heads_local, DK)
    value_heads = value_path.reshape(key_count, heads_local, DK)

    def score_block():
        raw = jnp.einsum("qhd,khd->hqk", query_heads, key_heads, preferred_element_type=jnp.float32)
        return raw + bias_local

    scores = score_block()
    row_max = jnp.max(scores, axis=-1, keepdims=True)
    raised = jnp.exp(scores - row_max)
    totals = jnp.sum(raised, axis=-1, keepdims=True)
    log_total = row_max + jnp.log(totals)
    attention = (raised / totals).astype(jnp.bfloat16)
    mixed = jnp.einsum("hqk,khd->qhd", attention, value_heads, preferred_element_type=jnp.float32)
    mixed = mixed.reshape(row_count, inner).astype(jnp.bfloat16)
    attended = lax.psum(
        jnp.dot(mixed, w_out, preferred_element_type=jnp.float32).astype(jnp.bfloat16), "tensor"
    ).astype(jnp.float32)
    middle = start_in + attended
    scale_two = lax.rsqrt(jnp.mean(middle * middle, axis=-1, keepdims=True) + norm_eps)
    normed_two = (middle * scale_two * gain_second).astype(jnp.bfloat16)
    gate_pre = jnp.dot(normed_two, w_gate, preferred_element_type=jnp.float32)
    up_pre = jnp.dot(normed_two, w_up, preferred_element_type=jnp.float32)
    activated = gelu_tanh(gate_pre)
    hidden = (activated * up_pre).astype(jnp.bfloat16)
    feed = lax.psum(
        jnp.dot(hidden, w_down, preferred_element_type=jnp.float32).astype(jnp.bfloat16), "tensor"
    ).astype(jnp.float32)
    produced = (middle + feed).astype(jnp.bfloat16)
    grad_out = grad_in.astype(jnp.float32)
    down_in = grad_out.astype(jnp.bfloat16)
    down_grad = left_dot(hidden, down_in)
    hidden_grad = right_dot(down_in, w_down)
    unused, gelu_pull = jax.vjp(gelu_tanh, gate_pre)
    gate_grad = gelu_pull(hidden_grad * up_pre)[0].astype(jnp.bfloat16)
    up_grad = (hidden_grad * activated).astype(jnp.bfloat16)
    gate_wgrad = left_dot(normed_two, gate_grad)
    up_wgrad = left_dot(normed_two, up_grad)
    normed_two_grad = lax.psum(
        (right_dot(gate_grad, w_gate) + right_dot(up_grad, w_up)).astype(jnp.bfloat16), "tensor"
    ).astype(jnp.float32)
    middle_part, gain_two_grad = norm_back(middle, scale_two, gain_second, normed_two_grad)
    middle_grad = grad_out + middle_part
    out_in = middle_grad.astype(jnp.bfloat16)
    out_wgrad = left_dot(mixed, out_in)
    mixed_grad = right_dot(out_in, w_out).astype(jnp.bfloat16)
    mixed_heads = mixed_grad.reshape(row_count, heads_local, DK)
    soft = jnp.exp(score_block() - log_total)
    soft_low = soft.astype(jnp.bfloat16)
    values_full = jnp.einsum(
        "hqk,qhd->khd", soft_low, mixed_heads, preferred_element_type=jnp.float32
    )
    weight_grad = jnp.einsum(
        "qhd,khd->hqk", mixed_heads, value_heads, preferred_element_type=jnp.float32
    )
    scores_grad = soft * (weight_grad - jnp.sum(weight_grad * soft, axis=-1, keepdims=True))
    scores_grad = scores_grad.astype(jnp.bfloat16)
    queries_grad = jnp.einsum(
        "hqk,khd->qhd", scores_grad, key_heads, preferred_element_type=jnp.float32
    )
    queries_grad = queries_grad.reshape(row_count, inner).astype(jnp.bfloat16)
    keys_full = jnp.einsum(
        "hqk,qhd->khd", scores_grad, query_heads, preferred_element_type=jnp.float32
    )
    keys_own, values_own = (
        lax.psum_scatter(
            keys_full.reshape(key_count, inner).astype(jnp.bfloat16),
            "ctx",
            scatter_dimension=0,
            tiled=True,
        ).astype(jnp.float32),
        lax.psum_scatter(
            values_full.reshape(key_count, inner).astype(jnp.bfloat16),
            "ctx",
            scatter_dimension=0,
            tiled=True,
        ).astype(jnp.float32),
    )
    keys_grad = keys_own.astype(jnp.bfloat16)
    values_grad = values_own.astype(jnp.bfloat16)
    query_wgrad = left_dot(normed_one, queries_grad)
    key_wgrad = left_dot(normed_one, keys_grad)
    value_wgrad = left_dot(normed_one, values_grad)
    local_first = (
        right_dot(queries_grad, w_query)
        + right_dot(keys_grad, w_key)
        + right_dot(values_grad, w_value)
    )
    normed_one_grad = lax.psum(local_first.astype(jnp.bfloat16), "tensor").astype(jnp.float32)
    input_part, gain_one_grad = norm_back(start_in, scale_one, gain_first, normed_one_grad)
    input_grad = (middle_grad + input_part).astype(jnp.bfloat16)
    grads = (
        gain_one_grad,
        query_wgrad,
        key_wgrad,
        value_wgrad,
        out_wgrad,
        gain_two_grad,
        gate_wgrad,
        up_wgrad,
        down_grad,
    )
    return (produced, input_grad, grads)


def on_device(
    inputs,
    cotangent,
    norm1_gain,
    w_query,
    w_key,
    w_value,
    w_out,
    norm2_gain,
    w_gate,
    w_up,
    w_down,
    bias_table,
):
    micro_count = inputs.shape[0]
    row_count = inputs.shape[1]
    key_count = row_count * lax.axis_size("ctx")
    heads_local = w_query.shape[1] // DK
    query_token = lax.axis_index("ctx") * row_count + jnp.arange(row_count, dtype=jnp.int32)
    key_token = jnp.arange(key_count, dtype=jnp.int32)
    table_local = lax.dynamic_slice_in_dim(
        bias_table, lax.axis_index("tensor") * heads_local, heads_local, 1
    )
    bias_local = score_bias(query_token, key_token, table_local, row_count // 5)
    outputs_list = []
    input_grads = []
    running = None
    for micro_step in range(micro_count):
        weights = (
            lax.all_gather(norm1_gain, "shard", axis=0, tiled=True),
            lax.all_gather(w_query, "shard", axis=0, tiled=True),
            lax.all_gather(w_key, "shard", axis=0, tiled=True),
            lax.all_gather(w_value, "shard", axis=0, tiled=True),
            lax.all_gather(w_out, "shard", axis=1, tiled=True),
            lax.all_gather(norm2_gain, "shard", axis=0, tiled=True),
            lax.all_gather(w_gate, "shard", axis=0, tiled=True),
            lax.all_gather(w_up, "shard", axis=0, tiled=True),
            lax.all_gather(w_down, "shard", axis=1, tiled=True),
        )
        produced, input_grad, grads = one_layer(
            weights, inputs[micro_step], cotangent[micro_step], bias_local, row_count, key_count
        )
        outputs_list.append(produced)
        input_grads.append(input_grad)
        running = grads if running is None else jax.tree.map(jnp.add, running, grads)
    owned = (
        lax.psum_scatter(
            running[0].astype(jnp.bfloat16), "shard", scatter_dimension=0, tiled=True
        ).astype(jnp.float32),
        lax.psum_scatter(
            running[1].astype(jnp.bfloat16), "shard", scatter_dimension=0, tiled=True
        ).astype(jnp.float32),
        lax.psum_scatter(
            running[2].astype(jnp.bfloat16), "shard", scatter_dimension=0, tiled=True
        ).astype(jnp.float32),
        lax.psum_scatter(
            running[3].astype(jnp.bfloat16), "shard", scatter_dimension=0, tiled=True
        ).astype(jnp.float32),
        lax.psum_scatter(
            running[4].astype(jnp.bfloat16), "shard", scatter_dimension=1, tiled=True
        ).astype(jnp.float32),
        lax.psum_scatter(
            running[5].astype(jnp.bfloat16), "shard", scatter_dimension=0, tiled=True
        ).astype(jnp.float32),
        lax.psum_scatter(
            running[6].astype(jnp.bfloat16), "shard", scatter_dimension=0, tiled=True
        ).astype(jnp.float32),
        lax.psum_scatter(
            running[7].astype(jnp.bfloat16), "shard", scatter_dimension=0, tiled=True
        ).astype(jnp.float32),
        lax.psum_scatter(
            running[8].astype(jnp.bfloat16), "shard", scatter_dimension=1, tiled=True
        ).astype(jnp.float32),
    )
    final_grads = jax.tree.map(
        lambda part: part.astype(jnp.float32), lax.psum(for_sending(owned), "ctx")
    )
    return (jnp.stack(outputs_list), jnp.stack(input_grads)) + tuple(final_grads)


def solution(mesh):
    placed = (
        P(None, ("shard", "ctx"), None),
        P(None, ("shard", "ctx"), None),
        P("shard"),
        P("shard", "tensor"),
        P("shard", "tensor"),
        P("shard", "tensor"),
        P("tensor", "shard"),
        P("shard"),
        P("shard", "tensor"),
        P("shard", "tensor"),
        P("tensor", "shard"),
        P(),
    )
    return jax.shard_map(
        on_device,
        mesh=mesh,
        in_specs=placed,
        out_specs=(
            P(None, ("shard", "ctx"), None),
            P(None, ("shard", "ctx"), None),
            P("shard"),
            P("shard", "tensor"),
            P("shard", "tensor"),
            P("shard", "tensor"),
            P("tensor", "shard"),
            P("shard"),
            P("shard", "tensor"),
            P("shard", "tensor"),
            P("tensor", "shard"),
        ),
        check_vma=False,
    )
```

profile of v0, /device:TPU:0, one launch (start us, length us, event | category | flops | bytes accessed | tf_op | source)
XLA Modules:
  0.0 1594.4 jit_solution(13874918093051243575)
XLA Ops:
  9.8 18.5 %all-gather = bf16[4,368,192]{1,2,0:T(8,128)(2,1)S(1)} all-gather(bf16[1,368,192]{1,2,0:T(8,128)(2,1)} %bitcast.319), channel_id=1, replica_groups=mesh['shard'=4,'ctx'=4,'tensor'=2] {'shard'}, dimensions={0}, use_global_device_ids=true | all-gather | bytes 706560 | tf_op jit(solution)/shard_map/all_gather | solution.py:231
  34.4 12.9 all-reduce.7
  47.4 15.8 all-gather.1
  67.4 14.9 all-gather.2
  83.9 8.6 all_gather.59
  93.0 151.6 %gather_fusion = f32[25600]{0:T(1024)S(1)} fusion(f32[32]{0:T(128)S(1)} %get-tuple-element.66, s32[25600]{0:T(1024)S(1)} %broadcast_clamp_fusion), kind=kCustom, calls=%fused_computation.clone | custom fusion | bytes 307200 | tf_op jit(solution)/shard_map/jit(_take)/gather | solution.py:48
  244.7 151.6 %gather_fusion.1 = f32[25600]{0:T(1024)S(1)} fusion(f32[32]{0:T(128)S(1)} %get-tuple-element.68, s32[25600]{0:T(1024)S(1)} %broadcast_clamp_fusion), kind=kCustom, calls=%fused_computation.1.clone | custom fusion | bytes 307200 | tf_op jit(solution)/shard_map/jit(_take)/gather | solution.py:48
  396.5 151.6 %gather_fusion.2 = f32[25600]{0:T(1024)S(1)} fusion(f32[32]{0:T(128)S(1)} %get-tuple-element.67, s32[25600]{0:T(1024)S(1)} %broadcast_clamp_fusion), kind=kCustom, calls=%fused_computation.2.clone | custom fusion | bytes 307200 | tf_op jit(solution)/shard_map/jit(_take)/gather | solution.py:48
  548.3 8.6 all_gather.60
  557.1 15.0 all-gather.3
  573.0 7.6 all_gather.50
  580.9 8.6 all_gather.53
  596.1 14.5 all-reduce.22.cloned.1.call-done
  614.3 77.8 %all-gather.8.cloned.1.call-done = bf16[1472,1792]{1,0:T(8,128)(2,1)} async-done(((bf16[368,1792]{1,0:T(8,128)(2,1)}), bf16[1472,1792]{1,0:T(8,128)(2,1)}) %all-gather.8.cloned.1.call-update) | async-done | bytes 5275664 | tf_op jit(solution)/shard_map/all_gather | solution.py:234
  692.2 4.3 fusion.158
  696.5 94.0 %all-gather.10.cloned.1.call-done = bf16[1472,1792]{1,0:T(8,128)(2,1)} async-done(((bf16[368,1792]{1,0:T(8,128)(2,1)}), bf16[1472,1792]{1,0:T(8,128)(2,1)}) %all-gather.10.cloned.1.call-update) | async-done | bytes 5275664 | tf_op jit(solution)/shard_map/all_gather | solution.py:235
  790.5 4.4 fusion.159
  794.9 1.8 fusion.156
  796.7 1.8 fusion.157
  798.5 90.3 %all-gather.12.cloned.1.call-done = bf16[1792,1472]{0,1:T(8,128)(2,1)} async-done(((bf16[1792,368]{0,1:T(8,128)(2,1)}), bf16[1792,1472]{0,1:T(8,128)(2,1)}) %all-gather.12.cloned.1.call-update) | async-done | bytes 5275664 | tf_op jit(solution)/shard_map/all_gather | solution.py:236
  888.8 4.7 multiply_convert_fusion
  893.6 4.4 fusion.162
  898.1 1.9 multiply_convert_fusion.1
  902.8 2.4 fusion.6
  905.1 2.4 fusion.4
  907.6 17.1 %all-reduce.20.cloned.1.call-done = (bf16[80,1472]{1,0:T(8,128)(2,1)}, bf16[80,1472]{1,0:T(8,128)(2,1)}) async-done(((bf16[80,1472]{1,0:T(8,128)(2,1)}, bf16[80,1472]{1,0:T(8,128)(2,1)}), (bf16[80,1472]{1,0:T(8,128)(2,1)}, bf16[80,1472]{1,0:T(8,128)(2,1)})) %all-reduce.20.cloned.1.call-update) | async-done | bytes 471056 | tf_op jit(solution)/shard_map/psum | solution.py:132
  924.8 2.1 fusion.53
  926.8 1.8 fusion.50
  941.2 1.7 convolution_convert_fusion.4
  947.9 1.9 fusion
  949.9 2.2 copy.77
  955.6 1.9 fusion.1
  957.4 2.2 copy.71
  959.7 1.7 reduce-scatter.34.cloned.1.call-done
  962.6 25.4 %reduce-scatter.38.cloned.1.call-done = bf16[80,192]{1,0:T(8,128)(2,1)} async-done(((bf16[320,192]{1,0:T(8,128)(2,1)}), bf16[80,192]{1,0:T(8,128)(2,1)}) %reduce-scatter.38.cloned.1.call-update) | async-done | bytes 30736
  988.0 2.0 fusion.2
  990.0 2.2 copy.73
  992.3 22.3 %reduce-scatter.36.cloned.1.call-done = bf16[80,192]{1,0:T(8,128)(2,1)} async-done(((bf16[320,192]{1,0:T(8,128)(2,1)}), bf16[80,192]{1,0:T(8,128)(2,1)}) %reduce-scatter.36.cloned.1.call-update) | async-done | bytes 30736
  1015.8 25.4 %reduce-scatter.40.cloned.1.call-done = bf16[80,192]{1,0:T(8,128)(2,1)} async-done(((bf16[320,192]{1,0:T(8,128)(2,1)}), bf16[80,192]{1,0:T(8,128)(2,1)}) %reduce-scatter.40.cloned.1.call-update) | async-done | bytes 30736
  1041.2 2.0 fusion.3
  1043.2 2.2 copy.75
  1045.5 2.6 fusion.164
  1048.1 4.0 add_convert_fusion.2
  1054.7 3.9 add_convert_fusion.1
  1061.1 3.9 add_convert_fusion
  1065.3 4.9 convolution_convert_fusion
  1070.2 5.0 convolution_convert_fusion.2
  1078.2 1.7 copy.78
  1079.9 11.6 reduce-scatter.42.cloned.1.call-done
  1091.5 1.7 copy.72
  1093.2 23.3 %reduce-scatter.44.cloned.1.call-done = bf16[368,192]{1,0:T(8,128)(2,1)} async-done(((bf16[1472,192]{1,0:T(8,128)(2,1)}), bf16[368,192]{1,0:T(8,128)(2,1)}) %reduce-scatter.44.cloned.1.call-update) | async-done | bytes 141328
  1116.6 1.7 copy.74
  1118.3 23.1 %reduce-scatter.46.cloned.1.call-done = bf16[368,192]{1,0:T(8,128)(2,1)} async-done(((bf16[1472,192]{1,0:T(8,128)(2,1)}), bf16[368,192]{1,0:T(8,128)(2,1)}) %reduce-scatter.46.cloned.1.call-update) | async-done | bytes 141328
  1141.4 1.7 copy.76
  1143.1 94.0 %reduce-scatter.28.cloned.1.call-done = bf16[368,1792]{1,0:T(8,128)(2,1)} async-done(((bf16[1472,1792]{1,0:T(8,128)(2,1)}), bf16[368,1792]{1,0:T(8,128)(2,1)}) %reduce-scatter.28.cloned.1.call-update) | async-done | bytes 1318928 | tf_op jit(solution)/shard_map/reduce_scatter | solution.py:263
  1237.2 97.0 %reduce-scatter.30.cloned.1.call-done = bf16[368,1792]{1,0:T(8,128)(2,1)} async-done(((bf16[1472,1792]{1,0:T(8,128)(2,1)}), bf16[368,1792]{1,0:T(8,128)(2,1)}) %reduce-scatter.30.cloned.1.call-update) | async-done | bytes 1318928 | tf_op jit(solution)/shard_map/reduce_scatter | solution.py:266
  1334.2 97.1 %reduce-scatter.32.cloned.1.call-done = bf16[1792,368]{0,1:T(8,128)(2,1)} async-done(((bf16[1792,1472]{0,1:T(8,128)(2,1)}), bf16[1792,368]{0,1:T(8,128)(2,1)}) %reduce-scatter.32.cloned.1.call-update) | async-done | bytes 1318928 | tf_op jit(solution)/shard_map/reduce_scatter | solution.py:269
  1432.0 22.5 %all-reduce.18.cloned.1.call-done = (bf16[80,1472]{1,0:T(8,128)(2,1)}, bf16[80,1472]{1,0:T(8,128)(2,1)}, bf16[80,1472]{1,0:T(8,128)(2,1)}, bf16[80,1472]{1,0:T(8,128)(2,1)}) async-done(((bf16[80,1472]{1,0:T(8,128)(2,1)}, bf16[80,1472]{1,0:T(8,128)(2,1)}, bf16[80,1472]{1,0:T(8,128)(2,1)}, bf16[80,1472]{1,0:T(8,128)(2,1)}), (bf16[80,1472]{1,0:T(8,128)(2,1)}, bf16[80,1472]{1,0:T(8,128)(2,1)}, ...) | async-done | bytes 942096 | tf_op jit(solution)/shard_map/psum | solution.py:119
  1455.9 12.2 all-reduce.6
  1468.3 10.1 all-reduce.4
  1479.5 2.0 fusion.85
  1483.2 90.6 %all-reduce.16.cloned.1.call-done = (bf16[368,192]{0,1:T(8,128)(2,1)}, bf16[368,192]{0,1:T(8,128)(2,1)}, bf16[368,192]{0,1:T(8,128)(2,1)}, bf16[192,368]{1,0:T(8...) async-done(((bf16[368,192]{0,1:T(8,128)(2,1)}, bf16[368,192]{0,1:T(8,128)(2,1)}, bf16[368,192]{0,1:T(8,128)(2,1)}, ...) | async-done | bytes 4522000 | tf_op jit(solution)/shard_map/psum | solution.py:274
  1573.8 1.8 convert_element_type.457
  1580.5 3.0 convert_element_type.467
  (297 shorter events, 72.5 us)
Async XLA Ops:
  8.0 84.6 %copy-start = (f32[32,6]{0,1:T(8,128)S(1)}, f32[32,6]{0,1:T(8,128)}, u32[]{:S(2)}) copy-start(f32[32,6]{0,1:T(8,128)} %param.25) | copy-start | bytes 2308
  8.0 56.7 %copy-start.5 = (bf16[2,80,1472]{2,1,0:T(8,128)(2,1)S(1)}, bf16[2,80,1472]{2,1,0:T(8,128)(2,1)}, u32[]{:S(2)}) copy-start(bf16[2,80,1472]{2,1,0:T(8,128)(2,1)} %param.14) | copy-start | bytes 1413124
  8.0 602.5 %all-reduce.22.cloned.1.call-start = ((), (), s32[]{:S(2)}) async-start(), calls=%async_computation.28 | async-start | bytes 983040 | tf_op jit(solution)/shard_map/psum | solution.py:109
  8.7 83.9 %copy-start.65 = (s32[80]{0:T(128)}, s32[80]{0:T(128)S(1)}, u32[]{:S(2)}) copy-start(s32[80]{0:T(128)S(1)} %fusion.138) | copy-start | bytes 964
  9.8 57.6 %copy-start.50 = (bf16[368,192]{0,1:T(8,128)(2,1)S(1)}, bf16[368,192]{0,1:T(8,128)(2,1)}, u32[]{:S(2)}) copy-start(bf16[368,192]{0,1:T(8,128)(2,1)} %param.18) | copy-start | bytes 423940
  29.2 54.0 %copy-start.17 = (bf16[1472,192]{0,1:T(8,128)(2,1)}, bf16[1472,192]{0,1:T(8,128)(2,1)S(1)}, u32[]{:S(2)}) copy-start(bf16[1472,192]{0,1:T(8,128)(2,1)S(1)} %reshape.446) | copy-start | bytes 1695748
  64.1 18.2 %copy-start.15 = (bf16[1472,192]{0,1:T(8,128)(2,1)}, bf16[1472,192]{0,1:T(8,128)(2,1)S(1)}, u32[]{:S(2)}) copy-start(bf16[1472,192]{0,1:T(8,128)(2,1)S(1)} %reshape.448) | copy-start | bytes 1695748
  64.7 179.9 %copy-start.57 = (f32[80]{0:T(128)}, f32[80]{0:T(128)S(1)}, u32[]{:S(2)}) copy-start(f32[80]{0:T(128)S(1)} %get-tuple-element.74) | copy-start | bytes 964
  64.7 179.9 %copy-start.59 = (f32[80]{0:T(128)}, f32[80]{0:T(128)S(1)}, u32[]{:S(2)}) copy-start(f32[80]{0:T(128)S(1)} %get-tuple-element.87) | copy-start | bytes 964
  83.2 9.5 copy-start.13
  92.6 498.0 %copy-start.37 = (bf16[320,192]{0,1:T(8,128)(2,1)}, bf16[320,192]{0,1:T(8,128)(2,1)S(1)}, u32[]{:S(2)}) copy-start(bf16[320,192]{0,1:T(8,128)(2,1)S(1)} %copy.58) | copy-start | bytes 368644
  396.4 160.6 %copy-start.51 = (bf16[192,368]{1,0:T(8,128)(2,1)S(1)}, bf16[192,368]{1,0:T(8,128)(2,1)}, u32[]{:S(2)}) copy-start(bf16[192,368]{1,0:T(8,128)(2,1)} %param.20) | copy-start | bytes 423940
  396.4 176.5 %copy-start.54 = (bf16[80,192]{1,0:T(8,128)(2,1)S(1)}, bf16[80,192]{1,0:T(8,128)(2,1)}, u32[]{:S(2)}) copy-start(bf16[80,192]{1,0:T(8,128)(2,1)} %convolution_convert_fusion.19) | copy-start | bytes 92164
  396.4 184.3 %copy-start.53 = (bf16[80,192]{1,0:T(8,128)(2,1)S(1)}, bf16[80,192]{1,0:T(8,128)(2,1)}, u32[]{:S(2)}) copy-start(bf16[80,192]{1,0:T(8,128)(2,1)} %convolution_convert_fusion.18) | copy-start | bytes 92164
  396.5 193.1 %copy-start.66 = (s32[80]{0:T(128)S(1)}, s32[80]{0:T(128)}, u32[]{:S(2)}) copy-start(s32[80]{0:T(128)} %copy-done.65) | copy-start | bytes 964
  548.1 41.8 %copy-start.61 = (s32[320]{0:T(512)S(1)}, s32[320]{0:T(512)}, u32[]{:S(2)}) copy-start(s32[320]{0:T(512)} %fusion.131) | copy-start | bytes 3844
  548.1 41.8 %copy-start.69 = (s32[80]{0:T(128)S(1)}, s32[80]{0:T(128)}, u32[]{:S(2)}) copy-start(s32[80]{0:T(128)} %get-tuple-element.89) | copy-start | bytes 964
  548.1 41.8 %copy-start.70 = (s32[80]{0:T(128)S(1)}, s32[80]{0:T(128)}, u32[]{:S(2)}) copy-start(s32[80]{0:T(128)} %get-tuple-element.90) | copy-start | bytes 964
  548.1 41.8 %copy-start.71 = (pred[320]{0:T(512)(128)(4,1)S(1)}, pred[320]{0:T(512)(128)(4,1)}, u32[]{:S(2)}) copy-start(pred[320]{0:T(512)(128)(4,1)} %broadcast_compare_fusion) | copy-start | bytes 964
  548.3 43.6 %copy-start.42 = (bf16[80,192]{0,1:T(8,128)(2,1)}, bf16[80,192]{0,1:T(8,128)(2,1)S(1)}, u32[]{:S(2)}) copy-start(bf16[80,192]{0,1:T(8,128)(2,1)S(1)} %copy.59) | copy-start | bytes 92164
  557.0 34.8 %copy-start.32 = (bf16[320,192]{0,1:T(8,128)(2,1)}, bf16[320,192]{0,1:T(8,128)(2,1)S(1)}, u32[]{:S(2)}) copy-start(bf16[320,192]{0,1:T(8,128)(2,1)S(1)} %copy.60) | copy-start | bytes 368644
  580.7 13.6 copy-start.38
  580.9 13.5 copy-start.43
  592.8 20.3 %copy-start.45 = (bf16[3,64,80]{2,1,0:T(8,128)(2,1)}, bf16[3,64,80]{2,1,0:T(8,128)(2,1)S(1)}, u32[]{:S(2)}) copy-start(bf16[3,64,80]{2,1,0:T(8,128)(2,1)S(1)} %convolution_convert_fusion.11) | copy-start | bytes 92164
  593.8 98.4 %all-gather.8.cloned.1.call-start = ((), (), s32[]{:S(2)}) async-start(), calls=%async_computation.11 | async-start | bytes 6594560 | tf_op jit(solution)/shard_map/all_gather | solution.py:234
  594.4 196.1 %all-gather.10.cloned.1.call-start = ((), (), s32[]{:S(2)}) async-start(), calls=%async_computation.12 | async-start | bytes 6594560 | tf_op jit(solution)/shard_map/all_gather | solution.py:235
  595.0 293.8 %all-gather.12.cloned.1.call-start = ((), (), s32[]{:S(2)}) async-start(), calls=%async_computation.13 | async-start | bytes 6594560 | tf_op jit(solution)/shard_map/all_gather | solution.py:236
  595.6 329.2 %all-reduce.20.cloned.1.call-start = ((), (), s32[]{:S(2)}) async-start(), calls=%async_computation.27 | async-start | bytes 983040 | tf_op jit(solution)/shard_map/psum | solution.py:132
  596.1 328.7 %copy-start.52 = (f32[1472]{0:T(1024)}, f32[1472]{0:T(1024)S(1)}, u32[]{:S(2)}) copy-start(f32[1472]{0:T(1024)S(1)} %convert_element_type.383) | copy-start | bytes 17668
  612.5 312.3 %copy-start.62 = (f32[80]{0:T(128)}, f32[80]{0:T(128)S(1)}, u32[]{:S(2)}) copy-start(f32[80]{0:T(128)S(1)} %get-tuple-element.76) | copy-start | bytes 964
  613.1 311.7 %copy-start.63 = (f32[80]{0:T(128)}, f32[80]{0:T(128)S(1)}, u32[]{:S(2)}) copy-start(f32[80]{0:T(128)S(1)} %get-tuple-element.78) | copy-start | bytes 964
  614.3 180.6 %copy-start.7 = (bf16[80,1472]{1,0:T(8,128)(2,1)}, bf16[80,1472]{1,0:T(8,128)(2,1)S(1)}, u32[]{:S(2)}) copy-start(bf16[80,1472]{1,0:T(8,128)(2,1)S(1)} %get-tuple-element.60) | copy-start | bytes 706564
  794.9 93.9 %copy-start.6 = (bf16[2,80,1472]{2,1,0:T(8,128)(2,1)S(1)}, bf16[2,80,1472]{2,1,0:T(8,128)(2,1)}, u32[]{:S(2)}) copy-start(bf16[2,80,1472]{2,1,0:T(8,128)(2,1)} %param.15) | copy-start | bytes 1413124
  888.8 9.2 copy-start.29
  893.6 9.1 copy-start.21
  902.7 22.0 %copy-start.9 = (bf16[80,1472]{1,0:T(8,128)(2,1)S(1)}, bf16[80,1472]{1,0:T(8,128)(2,1)}, u32[]{:S(2)}) copy-start(bf16[80,1472]{1,0:T(8,128)(2,1)} %get-tuple-element.47) | copy-start | bytes 706564
  902.7 22.0 %copy-start.11 = (bf16[80,1472]{1,0:T(8,128)(2,1)S(1)}, bf16[80,1472]{1,0:T(8,128)(2,1)}, u32[]{:S(2)}) copy-start(bf16[80,1472]{1,0:T(8,128)(2,1)} %get-tuple-element.48) | copy-start | bytes 706564
  907.5 53.9 %reduce-scatter.34.cloned.1.call-start = ((), (), s32[]{:S(2)}) async-start(), calls=%async_computation.17 | async-start | bytes 204800
  934.3 12.2 copy-start.30
  936.2 51.9 %reduce-scatter.38.cloned.1.call-start = ((), (), s32[]{:S(2)}) async-start(), calls=%async_computation.19 | async-start | bytes 204800
  936.2 15.9 copy-start.33
  941.1 73.5 %reduce-scatter.36.cloned.1.call-start = ((), (), s32[]{:S(2)}) async-start(), calls=%async_computation.18 | async-start | bytes 204800
  946.5 94.7 %reduce-scatter.40.cloned.1.call-start = ((), (), s32[]{:S(2)}) async-start(), calls=%async_computation.20 | async-start | bytes 204800
  947.7 13.8 copy-start.60
  947.7 130.5 %reduce-scatter.48.cloned.1.call-start = ((), (), s32[]{:S(2)}) async-start(), calls=%async_computation.24 | async-start | bytes 942080
  949.9 38.2 %copy-start.58 = (f32[80]{0:T(128)S(1)}, f32[80]{0:T(128)}, u32[]{:S(2)}) copy-start(f32[80]{0:T(128)} %copy-done.57) | copy-start | bytes 964
  952.1 139.5 %reduce-scatter.42.cloned.1.call-start = ((), (), s32[]{:S(2)}) async-start(), calls=%async_computation.21 | async-start | bytes 942080
  959.7 156.9 %reduce-scatter.44.cloned.1.call-start = ((), (), s32[]{:S(2)}) async-start(), calls=%async_computation.22 | async-start | bytes 942080
  992.2 149.2 %reduce-scatter.46.cloned.1.call-start = ((), (), s32[]{:S(2)}) async-start(), calls=%async_computation.23 | async-start | bytes 942080
  1045.5 191.7 %reduce-scatter.28.cloned.1.call-start = ((), (), s32[]{:S(2)}) async-start(), calls=%async_computation.14 | async-start | bytes 6594560 | tf_op jit(solution)/shard_map/reduce_scatter | solution.py:263
  1052.2 282.0 %reduce-scatter.30.cloned.1.call-start = ((), (), s32[]{:S(2)}) async-start(), calls=%async_computation.15 | async-start | bytes 6594560 | tf_op jit(solution)/shard_map/reduce_scatter | solution.py:266
  1058.5 372.8 %reduce-scatter.32.cloned.1.call-start = ((), (), s32[]{:S(2)}) async-start(), calls=%async_computation.16 | async-start | bytes 6594560 | tf_op jit(solution)/shard_map/reduce_scatter | solution.py:269
  1065.0 10.2 copy-start.16
  1065.0 10.2 copy-start.41
  1065.1 389.4 %all-reduce.18.cloned.1.call-start = ((), (), s32[]{:S(2)}) async-start(), calls=%async_computation.26 | async-start | bytes 1966080 | tf_op jit(solution)/shard_map/psum | solution.py:119
  1076.9 355.1 %copy-start.55 = (f32[1472]{0:T(1024)S(1)}, f32[1472]{0:T(1024)}, u32[]{:S(2)}) copy-start(f32[1472]{0:T(1024)} %get-tuple-element.14) | copy-start | bytes 17668
  1076.9 355.1 %copy-start.56 = (f32[1472]{0:T(1024)S(1)}, f32[1472]{0:T(1024)}, u32[]{:S(2)}) copy-start(f32[1472]{0:T(1024)} %get-tuple-element.23) | copy-start | bytes 17668
  1076.9 402.6 %copy-start.10 = (bf16[80,1472]{1,0:T(8,128)(2,1)S(1)}, bf16[80,1472]{1,0:T(8,128)(2,1)}, u32[]{:S(2)}) copy-start(bf16[80,1472]{1,0:T(8,128)(2,1)} %get-tuple-element.47) | copy-start | bytes 706564
  1076.9 402.6 %copy-start.12 = (bf16[80,1472]{1,0:T(8,128)(2,1)S(1)}, bf16[80,1472]{1,0:T(8,128)(2,1)}, u32[]{:S(2)}) copy-start(bf16[80,1472]{1,0:T(8,128)(2,1)} %get-tuple-element.48) | copy-start | bytes 706564
  1076.9 402.6 %copy-start.67 = (f32[80]{0:T(128)S(1)}, f32[80]{0:T(128)}, u32[]{:S(2)}) copy-start(f32[80]{0:T(128)} %get-tuple-element.73) | copy-start | bytes 964
  1076.9 402.6 %copy-start.68 = (f32[80]{0:T(128)S(1)}, f32[80]{0:T(128)}, u32[]{:S(2)}) copy-start(f32[80]{0:T(128)} %get-tuple-element.88) | copy-start | bytes 964
  1078.1 495.6 %all-reduce.16.cloned.1.call-start = ((), (), s32[]{:S(2)}) async-start(), calls=%async_computation.25 | async-start | bytes 9093120 | tf_op jit(solution)/shard_map/psum | solution.py:274
  1573.8 9.7 copy-start.36
  1573.8 11.4 copy-start.35
  (30 other events, 137.6 us)
Sparse Core Ops, SparseCore 0:
  593.9 16.6 all-reduce.21
  907.7 17.0 all-reduce.19
  936.3 25.1 reduce-scatter.33
  964.1 23.9 reduce-scatter.37
  990.6 23.9 reduce-scatter.35
  1017.2 23.9 reduce-scatter.39
  1043.5 22.9 reduce-scatter.47
  1069.4 22.0 reduce-scatter.41
  1094.4 22.1 reduce-scatter.43
  1119.3 22.0 reduce-scatter.45
  1143.7 93.3 reduce-scatter.27
  1239.3 94.7 reduce-scatter.29
  1336.5 94.7 reduce-scatter.31
  1434.3 20.1 all-reduce.17
  1460.2 113.4 all-reduce.15
Sparse Core Ops, SparseCore 1:
  595.8 96.3 all-gather.7
  693.6 96.8 all-gather.9
  791.9 96.8 all-gather.11
where the time goes:
time: 1600 us; the launch traced here: 1590 us
  waiting for transfers between devices  830 us (52%)
  local copies, waits for them, and re-layouts  489 us (31%)
  blocking collectives  133 us (8%)
  matrix products  91 us (6%)
  other arithmetic  32.1 us (2%)
  between operations  18.4 us (1%)
    gather x6, local copies, waits for them, and re-layouts, score_bias(): jnp.take(table[:, head], bucket, axis=0)  455 us
    unnamed x26, waiting for transfers between devices  135 us
    reduce_scatter x1, waiting for transfers between devices, on_device(): lax.psum_scatter(running[8].astype(jnp.bfloat16), 'shard', scatter_dimens...  97.1 us
    reduce_scatter x1, waiting for transfers between devices, on_device(): lax.psum_scatter(running[7].astype(jnp.bfloat16), 'shard', scatter_dimens...  97 us
    reduce_scatter x1, waiting for transfers between devices, on_device(): lax.psum_scatter(running[6].astype(jnp.bfloat16), 'shard', scatter_dimens...  94 us
    all_gather x1, waiting for transfers between devices, on_device(): lax.all_gather(w_up, 'shard', axis=0, tiled=True)  94 us
    psum x1, waiting for transfers between devices, on_device(): lax.psum(for_sending(owned), 'ctx')  90.6 us
    all_gather x1, waiting for transfers between devices, on_device(): lax.all_gather(w_down, 'shard', axis=1, tiled=True)  90.3 us
  transfers between devices with their start and end apart: 18, of which 17 were waited for; matrix products, arithmetic and copies ran while one was open for 6% of the time, Pallas kernels for 0%

commit v1 on v0

--- a/solution.py
+++ b/solution.py
@@ -7,6 +7,27 @@
 norm_eps = 1e-06
 distance_marks = (8, 12, 16, 23, 32, 46, 64, 91)
 masked_score = -1e30
+
+
+def ring_gather(x, axis, dim):
+    size, mine, width = (lax.axis_size(axis), lax.axis_index(axis), x.shape[dim])
+    forward = [(i, (i + 1) % size) for i in range(size)]
+    behind = [(i, (i - 1) % size) for i in range(size)]
+    result = jnp.zeros((*x.shape[:dim], size * width, *x.shape[dim + 1 :]), x.dtype)
+    result = lax.dynamic_update_slice_in_dim(result, x, mine * width, axis=dim)
+    from_left = from_right = x
+    half = size // 2
+    for lap in range(1, half + 1):
+        from_left = lax.ppermute(from_left, axis, forward)
+        result = lax.dynamic_update_slice_in_dim(
+            result, from_left, (mine - lap) % size * width, axis=dim
+        )
+        if lap < size - half:
+            from_right = lax.ppermute(from_right, axis, behind)
+            result = lax.dynamic_update_slice_in_dim(
+                result, from_right, (mine + lap) % size * width, axis=dim
+            )
+    return result
 
 
 def for_sending(x):
@@ -233,7 +254,7 @@
             lax.all_gather(norm2_gain, "shard", axis=0, tiled=True),
             lax.all_gather(w_gate, "shard", axis=0, tiled=True),
             lax.all_gather(w_up, "shard", axis=0, tiled=True),
-            lax.all_gather(w_down, "shard", axis=1, tiled=True),
+            ring_gather(w_down, "shard", 1),
         )
         produced, input_grad, grads = one_layer(
             weights, inputs[micro_step], cotangent[micro_step], bias_local, row_count, key_count

time: 1600 us -> 1560 us (0.975)
  waiting for transfers between devices: 830 us -> 767 us
  starting transfers between devices: 1.6 us -> 26 us
    ppermute x0 -> x3, waiting for transfers between devices: none -> 102 us  [the longest x2 84.2 us: ring_gather(): from_left = lax.ppermute(from_left, axis, forward)]
    all_gather x1 -> x0, waiting for transfers between devices: 90.3 us -> none  [on_device(): lax.all_gather(w_down, 'shard', axis=1, tiled=True)]
    all_gather x1, waiting for transfers between devices: 77.8 us -> 3.2 us  [on_device(): lax.all_gather(w_gate, 'shard', axis=0, tiled=True)]
    ppermute x0 -> x3, starting transfers between devices: none -> 24.9 us  [the longest x2 21.1 us: ring_gather(): from_left = lax.ppermute(from_left, axis, forward)]
    unnamed x26 -> x25, waiting for transfers between devices: 135 us -> 143 us
  transfers between devices with their start and end apart: 18 -> 20, of which waited for: 17 -> 19; matrix products, arithmetic and copies ran while one was open for 6% -> 6% of each run, Pallas kernels for 0% -> 0%
where the time goes in v1:
time: 1560 us; the launch traced here: 1550 us
  waiting for transfers between devices  767 us (49%)
  local copies, waits for them, and re-layouts  495 us (32%)
  blocking collectives  133 us (9%)
  matrix products  83.4 us (5%)
  other arithmetic  31.4 us (2%)
  starting transfers between devices  26 us (2%)
  between operations  18.1 us (1%)
    gather x6, local copies, waits for them, and re-layouts, score_bias(): jnp.take(table[:, head], bucket, axis=0)  455 us
    unnamed x25, waiting for transfers between devices  143 us
    reduce_scatter x1, waiting for transfers between devices, on_device(): lax.psum_scatter(running[8].astype(jnp.bfloat16), 'shard', scatter_dimens...  97.2 us
    reduce_scatter x1, waiting for transfers between devices, on_device(): lax.psum_scatter(running[7].astype(jnp.bfloat16), 'shard', scatter_dimens...  97 us
    all_gather x1, waiting for transfers between devices, on_device(): lax.all_gather(w_up, 'shard', axis=0, tiled=True)  94.5 us
    reduce_scatter x1, waiting for transfers between devices, on_device(): lax.psum_scatter(running[6].astype(jnp.bfloat16), 'shard', scatter_dimens...  94 us
    psum x1, waiting for transfers between devices, on_device(): lax.psum(for_sending(owned), 'ctx')  90.6 us
    ppermute x2, waiting for transfers between devices, ring_gather(): from_left = lax.ppermute(from_left, axis, forward)  84.2 us
  transfers between devices with their start and end apart: 20, of which 19 were waited for; matrix products, arithmetic and copies ran while one was open for 6% of the time, Pallas kernels for 0%

profile of v1, /device:TPU:0, one launch (start us, length us, event | category | flops | bytes accessed | tf_op | source)
XLA Modules:
  0.0 1554.0 jit_solution(17214918986755198946)
XLA Ops:
  9.2 18.5 %all-gather = bf16[4,368,192]{1,2,0:T(8,128)(2,1)S(1)} all-gather(bf16[1,368,192]{1,2,0:T(8,128)(2,1)} %bitcast.323), channel_id=1, replica_groups=mesh['shard'=4,'ctx'=4,'tensor'=2] {'shard'}, dimensions={0}, use_global_device_ids=true | all-gather | bytes 706560 | tf_op jit(solution)/shard_map/all_gather | solution.py:252
  33.9 12.3 all-reduce.7
  46.2 16.5 %all-gather.1 = bf16[4,368,192]{1,2,0:T(8,128)(2,1)S(1)} all-gather(bf16[1,368,192]{1,2,0:T(8,128)(2,1)} %bitcast.324), channel_id=1, replica_groups=mesh['shard'=4,'ctx'=4,'tensor'=2] {'shard'}, dimensions={0}, use_global_device_ids=true | all-gather | bytes 706560 | tf_op jit(solution)/shard_map/all_gather | solution.py:250
  65.6 14.9 all-gather.2
  82.1 8.6 all_gather.54
  91.3 151.6 %gather_fusion = f32[25600]{0:T(1024)S(1)} fusion(f32[32]{0:T(128)S(1)} %get-tuple-element.66, s32[25600]{0:T(1024)S(1)} %broadcast_clamp_fusion), kind=kCustom, calls=%fused_computation.clone | custom fusion | bytes 307200 | tf_op jit(solution)/shard_map/jit(_take)/gather | solution.py:69
  243.0 151.6 %gather_fusion.1 = f32[25600]{0:T(1024)S(1)} fusion(f32[32]{0:T(128)S(1)} %get-tuple-element.68, s32[25600]{0:T(1024)S(1)} %broadcast_clamp_fusion), kind=kCustom, calls=%fused_computation.1.clone | custom fusion | bytes 307200 | tf_op jit(solution)/shard_map/jit(_take)/gather | solution.py:69
  394.7 151.6 %gather_fusion.2 = f32[25600]{0:T(1024)S(1)} fusion(f32[32]{0:T(128)S(1)} %get-tuple-element.67, s32[25600]{0:T(1024)S(1)} %broadcast_clamp_fusion), kind=kCustom, calls=%fused_computation.2.clone | custom fusion | bytes 307200 | tf_op jit(solution)/shard_map/jit(_take)/gather | solution.py:69
  546.5 8.6 all_gather.55
  555.3 15.0 all-gather.3
  571.2 7.6 all_gather.46
  579.1 8.6 all_gather.49
  593.3 3.8 collective-permute-start.1
  597.1 2.8 broadcast.800
  599.9 2.6 constant_dynamic-update-slice_fusion.3
  602.4 5.9 all-reduce.22.cloned.1.call-done
  609.7 40.1 %collective-permute-done = bf16[1792,368]{0,1:T(8,128)(2,1)} collective-permute-done((bf16[1792,368]{0,1:T(8,128)(2,1)}, bf16[1792,368]{0,1:T(8,128)(2,1)}, u32[]{:S(2)}, u32[]{:S(2)}) %collective-permute-start) | collective-permute-done | bytes 1318944 | tf_op jit(solution)/shard_map/ppermute | solution.py:21
  649.8 21.0 %collective-permute-start.2 = (bf16[1792,368]{0,1:T(8,128)(2,1)}, bf16[1792,368]{0,1:T(8,128)(2,1)S(1)}, u32[]{:S(2)}, u32[]{:S(2)}) collective-permute-start(bf16[1792,368]{0,1:T(8,128)(2,1)} %collective-permute-done), channel_id=1, source_target_pairs={{0,8},{8,16},{16,24},{24,0},{1,9},{9,17},{17,25},{25,1},{2,10},{10... | collective-permute-start | bytes 3956744 | tf_op jit(solution)/shard_map/ppermute | solution.py:21
  673.2 2.6 constant_dynamic-update-slice_fusion.2
  675.7 18.1 %collective-permute-done.1 = bf16[1792,368]{0,1:T(8,128)(2,1)} collective-permute-done((bf16[1792,368]{0,1:T(8,128)(2,1)}, bf16[1792,368]{0,1:T(8,128)(2,1)}, u32[]{:S(2)}, u32[]{:S(2)}) %collective-permute-start.1) | collective-permute-done | bytes 1318944 | tf_op jit(solution)/shard_map/ppermute | solution.py:26
  693.8 2.5 constant_dynamic-update-slice_fusion.1
  696.3 44.1 %collective-permute-done.2 = bf16[1792,368]{0,1:T(8,128)(2,1)S(1)} collective-permute-done((bf16[1792,368]{0,1:T(8,128)(2,1)}, bf16[1792,368]{0,1:T(8,128)(2,1)S(1)}, u32[]{:S(2)}, u32[]{:S(2)}) %collective-permute-start.2) | collective-permute-done | bytes 1318944 | tf_op jit(solution)/shard_map/ppermute | solution.py:21
  741.6 3.2 all-gather.7.cloned.1.call-done
  744.8 4.3 fusion.156
  749.2 94.5 %all-gather.9.cloned.1.call-done = bf16[1472,1792]{1,0:T(8,128)(2,1)} async-done(((bf16[368,1792]{1,0:T(8,128)(2,1)}), bf16[1472,1792]{1,0:T(8,128)(2,1)}) %all-gather.9.cloned.1.call-update) | async-done | bytes 5275664 | tf_op jit(solution)/shard_map/all_gather | solution.py:256
  843.6 3.6 fusion.157
  847.3 4.9 multiply_convert_fusion
  854.3 4.4 multiply_convert_fusion.1
  862.1 2.4 fusion.6
  864.5 2.4 fusion.4
  866.9 17.2 %all-reduce.20.cloned.1.call-done = (bf16[80,1472]{1,0:T(8,128)(2,1)}, bf16[80,1472]{1,0:T(8,128)(2,1)}) async-done(((bf16[80,1472]{1,0:T(8,128)(2,1)}, bf16[80,1472]{1,0:T(8,128)(2,1)}), (bf16[80,1472]{1,0:T(8,128)(2,1)}, bf16[80,1472]{1,0:T(8,128)(2,1)})) %all-reduce.20.cloned.1.call-update) | async-done | bytes 471056 | tf_op jit(solution)/shard_map/psum | solution.py:153
  884.1 2.1 fusion.53
  886.2 1.8 fusion.50
  898.7 1.7 copy.67
  900.4 1.7 convolution_convert_fusion.4
  905.0 2.1 fusion.115
  912.7 8.0 reduce-scatter.34.cloned.1.call-done
  920.7 2.2 fusion.144
  922.9 25.0 %reduce-scatter.38.cloned.1.call-done = bf16[80,192]{1,0:T(8,128)(2,1)} async-done(((bf16[320,192]{1,0:T(8,128)(2,1)}), bf16[80,192]{1,0:T(8,128)(2,1)}) %reduce-scatter.38.cloned.1.call-update) | async-done | bytes 30736
  950.8 23.7 %reduce-scatter.36.cloned.1.call-done = bf16[80,192]{1,0:T(8,128)(2,1)} async-done(((bf16[320,192]{1,0:T(8,128)(2,1)}), bf16[80,192]{1,0:T(8,128)(2,1)}) %reduce-scatter.36.cloned.1.call-update) | async-done | bytes 30736
  974.5 2.2 fusion.146
  976.7 24.4 %reduce-scatter.40.cloned.1.call-done = bf16[80,192]{1,0:T(8,128)(2,1)} async-done(((bf16[320,192]{1,0:T(8,128)(2,1)}), bf16[80,192]{1,0:T(8,128)(2,1)}) %reduce-scatter.40.cloned.1.call-update) | async-done | bytes 30736
  1005.6 3.9 add_convert_fusion.2
  1012.1 4.0 add_convert_fusion.1
  1018.6 3.9 add_convert_fusion
  1022.8 4.9 convolution_convert_fusion
  1027.7 5.0 convolution_convert_fusion.2
  1035.7 1.7 copy.78
  1037.4 14.0 reduce-scatter.42.cloned.1.call-done
  1051.4 1.7 copy.72
  1053.1 23.3 %reduce-scatter.44.cloned.1.call-done = bf16[368,192]{1,0:T(8,128)(2,1)} async-done(((bf16[1472,192]{1,0:T(8,128)(2,1)}), bf16[368,192]{1,0:T(8,128)(2,1)}) %reduce-scatter.44.cloned.1.call-update) | async-done | bytes 141328
  1076.4 1.7 copy.74
  1078.1 23.1 %reduce-scatter.46.cloned.1.call-done = bf16[368,192]{1,0:T(8,128)(2,1)} async-done(((bf16[1472,192]{1,0:T(8,128)(2,1)}), bf16[368,192]{1,0:T(8,128)(2,1)}) %reduce-scatter.46.cloned.1.call-update) | async-done | bytes 141328
  1101.3 1.7 copy.76
  1103.0 94.0 %reduce-scatter.28.cloned.1.call-done = bf16[368,1792]{1,0:T(8,128)(2,1)} async-done(((bf16[1472,1792]{1,0:T(8,128)(2,1)}), bf16[368,1792]{1,0:T(8,128)(2,1)}) %reduce-scatter.28.cloned.1.call-update) | async-done | bytes 1318928 | tf_op jit(solution)/shard_map/reduce_scatter | solution.py:284
  1197.0 97.0 %reduce-scatter.30.cloned.1.call-done = bf16[368,1792]{1,0:T(8,128)(2,1)} async-done(((bf16[1472,1792]{1,0:T(8,128)(2,1)}), bf16[368,1792]{1,0:T(8,128)(2,1)}) %reduce-scatter.30.cloned.1.call-update) | async-done | bytes 1318928 | tf_op jit(solution)/shard_map/reduce_scatter | solution.py:287
  1294.0 97.2 %reduce-scatter.32.cloned.1.call-done = bf16[1792,368]{0,1:T(8,128)(2,1)} async-done(((bf16[1792,1472]{0,1:T(8,128)(2,1)}), bf16[1792,368]{0,1:T(8,128)(2,1)}) %reduce-scatter.32.cloned.1.call-update) | async-done | bytes 1318928 | tf_op jit(solution)/shard_map/reduce_scatter | solution.py:290
  1391.9 22.4 %all-reduce.18.cloned.1.call-done = (bf16[80,1472]{1,0:T(8,128)(2,1)}, bf16[80,1472]{1,0:T(8,128)(2,1)}, bf16[80,1472]{1,0:T(8,128)(2,1)}, bf16[80,1472]{1,0:T(8,128)(2,1)}) async-done(((bf16[80,1472]{1,0:T(8,128)(2,1)}, bf16[80,1472]{1,0:T(8,128)(2,1)}, bf16[80,1472]{1,0:T(8,128)(2,1)}, bf16[80,1472]{1,0:T(8,128)(2,1)}), (bf16[80,1472]{1,0:T(8,128)(2,1)}, bf16[80,1472]{1,0:T(8,128)(2,1)}, ...) | async-done | bytes 942096 | tf_op jit(solution)/shard_map/psum | solution.py:140
  1415.8 12.2 all-reduce.6
  1428.1 10.1 all-reduce.4
  1439.4 2.0 fusion.85
  1443.0 90.6 %all-reduce.16.cloned.1.call-done = (bf16[368,192]{0,1:T(8,128)(2,1)}, bf16[368,192]{0,1:T(8,128)(2,1)}, bf16[368,192]{0,1:T(8,128)(2,1)}, bf16[192,368]{1,0:T(8...) async-done(((bf16[368,192]{0,1:T(8,128)(2,1)}, bf16[368,192]{0,1:T(8,128)(2,1)}, bf16[368,192]{0,1:T(8,128)(2,1)}, ...) | async-done | bytes 4522000 | tf_op jit(solution)/shard_map/psum | solution.py:295
  1533.6 1.8 convert_element_type.457
  1540.3 3.0 convert_element_type.467
  (281 shorter events, 76.2 us)
Async XLA Ops:
  8.0 82.9 %copy-start = (f32[32,6]{0,1:T(8,128)S(1)}, f32[32,6]{0,1:T(8,128)}, u32[]{:S(2)}) copy-start(f32[32,6]{0,1:T(8,128)} %param.25) | copy-start | bytes 2308
  8.0 56.2 %copy-start.2 = (bf16[2,80,1472]{2,1,0:T(8,128)(2,1)S(1)}, bf16[2,80,1472]{2,1,0:T(8,128)(2,1)}, u32[]{:S(2)}) copy-start(bf16[2,80,1472]{2,1,0:T(8,128)(2,1)} %param.14) | copy-start | bytes 1413124
  8.0 600.3 %all-reduce.22.cloned.1.call-start = ((), (), s32[]{:S(2)}) async-start(), calls=%async_computation.27 | async-start | bytes 983040 | tf_op jit(solution)/shard_map/psum | solution.py:130
  8.2 82.7 %copy-start.53 = (s32[80]{0:T(128)}, s32[80]{0:T(128)S(1)}, u32[]{:S(2)}) copy-start(s32[80]{0:T(128)S(1)} %fusion.136) | copy-start | bytes 964
  9.2 56.3 %copy-start.42 = (bf16[368,192]{0,1:T(8,128)(2,1)S(1)}, bf16[368,192]{0,1:T(8,128)(2,1)}, u32[]{:S(2)}) copy-start(bf16[368,192]{0,1:T(8,128)(2,1)} %param.18) | copy-start | bytes 423940
  28.6 52.8 %copy-start.14 = (bf16[1472,192]{0,1:T(8,128)(2,1)}, bf16[1472,192]{0,1:T(8,128)(2,1)S(1)}, u32[]{:S(2)}) copy-start(bf16[1472,192]{0,1:T(8,128)(2,1)S(1)} %reshape.446) | copy-start | bytes 1695748
  63.6 16.9 %copy-start.12 = (bf16[1472,192]{0,1:T(8,128)(2,1)}, bf16[1472,192]{0,1:T(8,128)(2,1)S(1)}, u32[]{:S(2)}) copy-start(bf16[1472,192]{0,1:T(8,128)(2,1)S(1)} %reshape.448) | copy-start | bytes 1695748
  64.2 178.7 %copy-start.47 = (f32[80]{0:T(128)}, f32[80]{0:T(128)S(1)}, u32[]{:S(2)}) copy-start(f32[80]{0:T(128)S(1)} %get-tuple-element.74) | copy-start | bytes 964
  64.2 178.7 %copy-start.49 = (f32[80]{0:T(128)}, f32[80]{0:T(128)S(1)}, u32[]{:S(2)}) copy-start(f32[80]{0:T(128)S(1)} %get-tuple-element.87) | copy-start | bytes 964
  81.4 9.5 copy-start.10
  90.8 497.9 %copy-start.32 = (bf16[320,192]{0,1:T(8,128)(2,1)}, bf16[320,192]{0,1:T(8,128)(2,1)S(1)}, u32[]{:S(2)}) copy-start(bf16[320,192]{0,1:T(8,128)(2,1)S(1)} %copy.58) | copy-start | bytes 368644
  394.7 160.6 %copy-start.43 = (bf16[192,368]{1,0:T(8,128)(2,1)S(1)}, bf16[192,368]{1,0:T(8,128)(2,1)}, u32[]{:S(2)}) copy-start(bf16[192,368]{1,0:T(8,128)(2,1)} %param.20) | copy-start | bytes 423940
  394.7 193.1 %copy-start.54 = (s32[80]{0:T(128)S(1)}, s32[80]{0:T(128)}, u32[]{:S(2)}) copy-start(s32[80]{0:T(128)} %copy-done.53) | copy-start | bytes 964
  546.3 41.8 %copy-start.57 = (s32[80]{0:T(128)S(1)}, s32[80]{0:T(128)}, u32[]{:S(2)}) copy-start(s32[80]{0:T(128)} %get-tuple-element.89) | copy-start | bytes 964
  546.3 41.8 %copy-start.58 = (s32[80]{0:T(128)S(1)}, s32[80]{0:T(128)}, u32[]{:S(2)}) copy-start(s32[80]{0:T(128)} %get-tuple-element.90) | copy-start | bytes 964
  546.3 41.8 %copy-start.59 = (pred[320]{0:T(512)(128)(4,1)S(1)}, pred[320]{0:T(512)(128)(4,1)}, u32[]{:S(2)}) copy-start(pred[320]{0:T(512)(128)(4,1)} %broadcast_compare_fusion) | copy-start | bytes 964
  546.5 43.5 %copy-start.34 = (bf16[80,192]{0,1:T(8,128)(2,1)}, bf16[80,192]{0,1:T(8,128)(2,1)S(1)}, u32[]{:S(2)}) copy-start(bf16[80,192]{0,1:T(8,128)(2,1)S(1)} %copy.59) | copy-start | bytes 92164
  555.2 35.7 %copy-start.26 = (bf16[320,192]{0,1:T(8,128)(2,1)}, bf16[320,192]{0,1:T(8,128)(2,1)S(1)}, u32[]{:S(2)}) copy-start(bf16[320,192]{0,1:T(8,128)(2,1)S(1)} %copy.60) | copy-start | bytes 368644
  578.9 13.6 copy-start.33
  579.0 13.5 copy-start.35
  591.0 11.5 copy-start.37
  592.0 152.9 %all-gather.7.cloned.1.call-start = ((), (), s32[]{:S(2)}) async-start(), calls=%async_computation.11 | async-start | bytes 6594560 | tf_op jit(solution)/shard_map/all_gather | solution.py:255
  592.6 251.1 %all-gather.9.cloned.1.call-start = ((), (), s32[]{:S(2)}) async-start(), calls=%async_computation.12 | async-start | bytes 6594560 | tf_op jit(solution)/shard_map/all_gather | solution.py:256
  593.1 291.0 %all-reduce.20.cloned.1.call-start = ((), (), s32[]{:S(2)}) async-start(), calls=%async_computation.26 | async-start | bytes 983040 | tf_op jit(solution)/shard_map/psum | solution.py:153
  593.2 56.6 %collective-permute-start = (bf16[1792,368]{0,1:T(8,128)(2,1)}, bf16[1792,368]{0,1:T(8,128)(2,1)}, u32[]{:S(2)}, u32[]{:S(2)}) collective-permute-start(bf16[1792,368]{0,1:T(8,128)(2,1)} %param.24), channel_id=1, source_target_pairs={{0,8},{8,16},{16,24},{24,0},{1,9},{9,17},{17,25},{25,1},{2,10},{10... | collective-permute-start | bytes 3956744 | tf_op jit(solution)/shard_map/ppermute | solution.py:21
  593.3 100.6 %collective-permute-start.1 = (bf16[1792,368]{0,1:T(8,128)(2,1)}, bf16[1792,368]{0,1:T(8,128)(2,1)}, u32[]{:S(2)}, u32[]{:S(2)}) collective-permute-start(bf16[1792,368]{0,1:T(8,128)(2,1)} %param.24), channel_id=1, source_target_pairs={{0,24},{8,0},{16,8},{24,16},{1,25},{9,1},{17,9},{25,17},{2,26},{10... | collective-permute-start | bytes 3956744 | tf_op jit(solution)/shard_map/ppermute | solution.py:26
  597.1 287.0 %copy-start.44 = (f32[1472]{0:T(1024)}, f32[1472]{0:T(1024)S(1)}, u32[]{:S(2)}) copy-start(f32[1472]{0:T(1024)S(1)} %convert_element_type.383) | copy-start | bytes 17668
  649.8 90.6 %collective-permute-start.2 = (bf16[1792,368]{0,1:T(8,128)(2,1)}, bf16[1792,368]{0,1:T(8,128)(2,1)S(1)}, u32[]{:S(2)}, u32[]{:S(2)}) collective-permute-start(bf16[1792,368]{0,1:T(8,128)(2,1)} %collective-permute-done), channel_id=1, source_target_pairs={{0,8},{8,16},{16,24},{24,0},{1,9},{9,17},{17,25},{25,1},{2,10},{10... | collective-permute-start | bytes 3956744 | tf_op jit(solution)/shard_map/ppermute | solution.py:21
  671.3 212.8 %copy-start.51 = (f32[80]{0:T(128)}, f32[80]{0:T(128)S(1)}, u32[]{:S(2)}) copy-start(f32[80]{0:T(128)S(1)} %get-tuple-element.76) | copy-start | bytes 964
  671.9 212.2 %copy-start.52 = (f32[80]{0:T(128)}, f32[80]{0:T(128)S(1)}, u32[]{:S(2)}) copy-start(f32[80]{0:T(128)S(1)} %get-tuple-element.78) | copy-start | bytes 964
  673.1 170.5 %copy-start.4 = (bf16[80,1472]{1,0:T(8,128)(2,1)}, bf16[80,1472]{1,0:T(8,128)(2,1)S(1)}, u32[]{:S(2)}) copy-start(bf16[80,1472]{1,0:T(8,128)(2,1)S(1)} %get-tuple-element.60) | copy-start | bytes 706564
  744.8 102.5 %copy-start.3 = (bf16[2,80,1472]{2,1,0:T(8,128)(2,1)S(1)}, bf16[2,80,1472]{2,1,0:T(8,128)(2,1)}, u32[]{:S(2)}) copy-start(bf16[2,80,1472]{2,1,0:T(8,128)(2,1)} %param.15) | copy-start | bytes 1413124
  843.6 8.6 slice-start
  843.6 9.6 slice-start.2
  852.2 9.8 copy-start.18
  862.1 22.1 %copy-start.6 = (bf16[80,1472]{1,0:T(8,128)(2,1)S(1)}, bf16[80,1472]{1,0:T(8,128)(2,1)}, u32[]{:S(2)}) copy-start(bf16[80,1472]{1,0:T(8,128)(2,1)} %get-tuple-element.47) | copy-start | bytes 706564
  862.1 22.1 %copy-start.8 = (bf16[80,1472]{1,0:T(8,128)(2,1)S(1)}, bf16[80,1472]{1,0:T(8,128)(2,1)}, u32[]{:S(2)}) copy-start(bf16[80,1472]{1,0:T(8,128)(2,1)} %get-tuple-element.48) | copy-start | bytes 706564
  866.9 53.9 %reduce-scatter.34.cloned.1.call-start = ((), (), s32[]{:S(2)}) async-start(), calls=%async_computation.16 | async-start | bytes 204800
  895.5 52.4 %reduce-scatter.38.cloned.1.call-start = ((), (), s32[]{:S(2)}) async-start(), calls=%async_computation.18 | async-start | bytes 204800
  895.5 14.7 copy-start.27
  896.9 13.8 copy-start.50
  900.4 10.7 copy-start.48
  900.4 74.1 %reduce-scatter.36.cloned.1.call-start = ((), (), s32[]{:S(2)}) async-start(), calls=%async_computation.17 | async-start | bytes 204800
  905.0 96.1 %reduce-scatter.40.cloned.1.call-start = ((), (), s32[]{:S(2)}) async-start(), calls=%async_computation.19 | async-start | bytes 204800
  907.1 128.6 %reduce-scatter.48.cloned.1.call-start = ((), (), s32[]{:S(2)}) async-start(), calls=%async_computation.23 | async-start | bytes 942080
  910.2 141.2 %reduce-scatter.42.cloned.1.call-start = ((), (), s32[]{:S(2)}) async-start(), calls=%async_computation.20 | async-start | bytes 942080
  912.6 91.4 %copy-start.25 = (bf16[80,1792]{1,0:T(8,128)(2,1)S(1)}, bf16[80,1792]{1,0:T(8,128)(2,1)}, u32[]{:S(2)}) copy-start(bf16[80,1792]{1,0:T(8,128)(2,1)} %copy-done.24) | copy-start | bytes 860164
  912.7 163.8 %reduce-scatter.44.cloned.1.call-start = ((), (), s32[]{:S(2)}) async-start(), calls=%async_computation.21 | async-start | bytes 942080
  950.8 150.5 %reduce-scatter.46.cloned.1.call-start = ((), (), s32[]{:S(2)}) async-start(), calls=%async_computation.22 | async-start | bytes 942080
  1003.9 193.1 %reduce-scatter.28.cloned.1.call-start = ((), (), s32[]{:S(2)}) async-start(), calls=%async_computation.13 | async-start | bytes 6594560 | tf_op jit(solution)/shard_map/reduce_scatter | solution.py:284
  1009.6 284.5 %reduce-scatter.30.cloned.1.call-start = ((), (), s32[]{:S(2)}) async-start(), calls=%async_computation.14 | async-start | bytes 6594560 | tf_op jit(solution)/shard_map/reduce_scatter | solution.py:287
  1016.1 375.1 %reduce-scatter.32.cloned.1.call-start = ((), (), s32[]{:S(2)}) async-start(), calls=%async_computation.15 | async-start | bytes 6594560 | tf_op jit(solution)/shard_map/reduce_scatter | solution.py:290
  1022.5 10.2 copy-start.13
  1022.5 391.8 %all-reduce.18.cloned.1.call-start = ((), (), s32[]{:S(2)}) async-start(), calls=%async_computation.25 | async-start | bytes 1966080 | tf_op jit(solution)/shard_map/psum | solution.py:140
  1027.7 6.9 copy-start.39
  1034.4 357.5 %copy-start.45 = (f32[1472]{0:T(1024)S(1)}, f32[1472]{0:T(1024)}, u32[]{:S(2)}) copy-start(f32[1472]{0:T(1024)} %get-tuple-element.14) | copy-start | bytes 17668
  1034.4 357.5 %copy-start.46 = (f32[1472]{0:T(1024)S(1)}, f32[1472]{0:T(1024)}, u32[]{:S(2)}) copy-start(f32[1472]{0:T(1024)} %get-tuple-element.23) | copy-start | bytes 17668
  1034.4 405.0 %copy-start.7 = (bf16[80,1472]{1,0:T(8,128)(2,1)S(1)}, bf16[80,1472]{1,0:T(8,128)(2,1)}, u32[]{:S(2)}) copy-start(bf16[80,1472]{1,0:T(8,128)(2,1)} %get-tuple-element.47) | copy-start | bytes 706564
  1034.4 405.0 %copy-start.9 = (bf16[80,1472]{1,0:T(8,128)(2,1)S(1)}, bf16[80,1472]{1,0:T(8,128)(2,1)}, u32[]{:S(2)}) copy-start(bf16[80,1472]{1,0:T(8,128)(2,1)} %get-tuple-element.48) | copy-start | bytes 706564
  1034.4 405.0 %copy-start.55 = (f32[80]{0:T(128)S(1)}, f32[80]{0:T(128)}, u32[]{:S(2)}) copy-start(f32[80]{0:T(128)} %get-tuple-element.73) | copy-start | bytes 964
  1034.4 405.0 %copy-start.56 = (f32[80]{0:T(128)S(1)}, f32[80]{0:T(128)}, u32[]{:S(2)}) copy-start(f32[80]{0:T(128)} %get-tuple-element.88) | copy-start | bytes 964
  1035.6 498.0 %all-reduce.16.cloned.1.call-start = ((), (), s32[]{:S(2)}) async-start(), calls=%async_computation.24 | async-start | bytes 9093120 | tf_op jit(solution)/shard_map/psum | solution.py:295
  1533.6 9.7 copy-start.31
  1533.6 11.4 copy-start.30
  (20 other events, 84.1 us)
Sparse Core Ops, SparseCore 0:
  592.1 16.1 all-reduce.21
  867.0 17.0 all-reduce.19
  895.6 25.1 reduce-scatter.33
  923.9 23.9 reduce-scatter.37
  950.5 23.9 reduce-scatter.35
  977.1 23.9 reduce-scatter.39
  1003.4 22.9 reduce-scatter.47
  1029.3 22.1 reduce-scatter.41
  1054.3 22.0 reduce-scatter.43
  1079.2 22.0 reduce-scatter.45
  1103.6 93.3 reduce-scatter.27
  1199.2 94.7 reduce-scatter.29
  1296.3 94.8 reduce-scatter.31
  1394.2 20.0 all-reduce.17
  1420.1 113.4 all-reduce.15
Sparse Core Ops, SparseCore 1:
  594.0 150.8 all-gather.6
  746.2 97.3 all-gather.8
